TPU v7x, 256 devices: a whole 4x4x8 slice. The times are simulated.
256 devices in a mesh: row: 32 (over z_hi, x, core), col: 8 (over y, z_lo).
Axes of the slice: x: 4, y: 4, z: 8 (z_hi: 4, z_lo: 2; z = z_hi * 2 + z_lo), core: 2. Of those that a mesh axis runs over, the one named last changes fastest.
Arguments:
- ocean_field: bfloat16 [32, 2048, 2048], P(None, 'row', 'col'), may hold values from -6 to 6
- cotangent: bfloat16 [2048, 2048], P('row', 'col'), may hold values from -6 to 6
- conv_weight: bfloat16 [3, 3, 32, 32], replicated, may hold values from -0.375 to 0.375
- conv_bias: float32 [32], replicated, may hold values from -3 to 3
- projection: float32 [32], replicated, may hold values from -4 to 4
- mode_weight: bfloat16 [128, 2, 32, 32, 256], P('row', None, None, None, 'col'), may hold values from -4.5 to 4.5
Outputs:
- grad_input: float32 [32, 2048, 2048], P(None, 'row', 'col')
- grad_spec: float32 [128, 2, 32, 32, 256], P('row', None, None, None, 'col')
- grad_conv: float32 [3, 3, 32, 32], replicated
- grad_bias: float32 [32], replicated
- grad_proj: float32 [32], replicated
All inputs are finite; a program needn't handle non-finite values.
Results may differ from a plain program's by a relative error of at most 0.0062.
Values may be sent and summed in bfloat16 or wider, within the bound.
A program may use at most 128 MiB of HBM per device.

v0:
```python
import math
import jax
import jax.numpy as jnp
from jax import lax
from jax.sharding import PartitionSpec as P

TWO_PI = 2.0 * math.pi
HIGH = lax.Precision.HIGHEST


def with_halo(array, sides, width):
    for axis, dim in sides:
        devices, length = (lax.axis_size(axis), array.shape[dim])
        up = [(i, (i + 1) % devices) for i in range(devices - 1)]
        down = [(j, i) for i, j in up]
        last = lax.slice_in_dim(array, length - width, length, axis=dim)
        first = lax.slice_in_dim(array, 0, width, axis=dim)
        before = lax.ppermute(last, axis, up)
        after = lax.ppermute(first, axis, down)
        array = jnp.concatenate([before, array, after], axis=dim)
    return array


def angle_pair(products, period):
    angles = (products % period).astype(jnp.float32) * (TWO_PI / period)
    return (jnp.cos(angles).astype(jnp.bfloat16), jnp.sin(angles).astype(jnp.bfloat16))


def column_table(col_ids, modes, period):
    freqs = jnp.arange(modes, dtype=jnp.int32)
    cosine, sine = angle_pair(freqs[:, None] * col_ids[None, :], period)
    return jnp.stack([cosine, -sine], axis=1)


def row_tables(row_ids, kx_ids, modes, period):
    freqs = jnp.where(kx_ids < modes, kx_ids, kx_ids - 2 * modes) % period
    return angle_pair(row_ids[:, None] * freqs[None, :], period)


def column_section(field, col_ids, modes, period):
    table = column_table(col_ids, modes, period)
    return jnp.einsum("cxy,kpy->kpcx", field, table, preferred_element_type=jnp.float32)


def row_section(partial_value, row_ids, kx_ids, modes, period):
    cosine, sine = row_tables(row_ids, kx_ids, modes, period)
    with_cos = jnp.einsum(
        "kpcx,xj->kpcj", partial_value, cosine.astype(jnp.float32), precision=HIGH
    )
    with_sin = jnp.einsum("kpcx,xj->kpcj", partial_value, sine.astype(jnp.float32), precision=HIGH)
    return jnp.stack([with_cos[:, 0] + with_sin[:, 1], with_cos[:, 1] - with_sin[:, 0]], axis=1)


def row_inverse(spectral, row_ids, kx_ids, modes, period):
    cosine, sine = row_tables(row_ids, kx_ids, modes, period)
    with_cos = jnp.einsum("kpcj,xj->kpcx", spectral, cosine, preferred_element_type=jnp.float32)
    with_sin = jnp.einsum("kpcj,xj->kpcx", spectral, sine, preferred_element_type=jnp.float32)
    return jnp.stack([with_cos[:, 0] - with_sin[:, 1], with_cos[:, 1] + with_sin[:, 0]], axis=1)


def column_inverse(summed, weights_ky, col_ids, modes, period, scale):
    table = column_table(col_ids, modes, period).astype(jnp.float32)
    weighted = summed * weights_ky[:, None, None, None]
    return scale * jnp.einsum("kpcx,kpy->cxy", weighted, table, precision=HIGH)


def mix_modes(spectrum, weight):
    wf = weight.astype(jnp.float32)
    real_part = jnp.einsum("kij,kioj->koj", spectrum[:, 0], wf[:, 0], precision=HIGH) - jnp.einsum(
        "kij,kioj->koj", spectrum[:, 1], wf[:, 1], precision=HIGH
    )
    imag_part = jnp.einsum("kij,kioj->koj", spectrum[:, 1], wf[:, 0], precision=HIGH) + jnp.einsum(
        "kij,kioj->koj", spectrum[:, 0], wf[:, 1], precision=HIGH
    )
    return jnp.stack([real_part, imag_part], axis=1)


def mix_back(spectrum, weight, grad_mixed):
    wf = weight.astype(jnp.float32)
    spec_re, spec_im = (spectrum[:, 0], spectrum[:, 1])
    grad_re, grad_im = (grad_mixed[:, 0], grad_mixed[:, 1])
    weight_re = (
        grad_re[:, None, :, :] * spec_re[:, :, None, :]
        + grad_im[:, None, :, :] * spec_im[:, :, None, :]
    )
    weight_im = (
        grad_im[:, None, :, :] * spec_re[:, :, None, :]
        - grad_re[:, None, :, :] * spec_im[:, :, None, :]
    )
    back_re = jnp.einsum("kioj,koj->kij", wf[:, 0], grad_re, precision=HIGH) + jnp.einsum(
        "kioj,koj->kij", wf[:, 1], grad_im, precision=HIGH
    )
    back_im = jnp.einsum("kioj,koj->kij", wf[:, 0], grad_im, precision=HIGH) - jnp.einsum(
        "kioj,koj->kij", wf[:, 1], grad_re, precision=HIGH
    )
    return (
        jnp.stack([weight_re, weight_im], axis=1),
        jnp.stack([back_re, back_im], axis=1).astype(jnp.bfloat16),
    )


def gelu_parts(pre):
    cdf = 0.5 * (1.0 + jax.scipy.special.erf(pre / math.sqrt(2.0)))
    pdf = jnp.exp(-0.5 * pre * pre) / math.sqrt(TWO_PI)
    return (pre * cdf, cdf + pre * pdf)


def conv_cells(padded, kernel, n_rows, n_cols):
    result = jnp.zeros((kernel.shape[3], n_rows, n_cols), jnp.float32)
    for tap_row in range(3):
        for tap_col in range(3):
            shifted = padded[:, tap_row : tap_row + n_rows, tap_col : tap_col + n_cols]
            result = result + jnp.einsum(
                "io,ixy->oxy", kernel[tap_row, tap_col], shifted, preferred_element_type=jnp.float32
            )
    return result


def conv_transpose(padded, kernel, n_rows, n_cols):
    result = jnp.zeros((kernel.shape[2], n_rows, n_cols), jnp.float32)
    for tap_row in range(3):
        for tap_col in range(3):
            shifted = padded[
                :, 2 - tap_row : 2 - tap_row + n_rows, 2 - tap_col : 2 - tap_col + n_cols
            ]
            result = result + jnp.einsum(
                "io,oxy->ixy", kernel[tap_row, tap_col], shifted, preferred_element_type=jnp.float32
            )
    return result


def kernel_grad(padded, grad_round, n_rows, n_cols):
    taps = []
    for tap_row in range(3):
        for tap_col in range(3):
            shifted = padded[:, tap_row : tap_row + n_rows, tap_col : tap_col + n_cols]
            taps.append(
                jnp.einsum("ixy,oxy->io", shifted, grad_round, preferred_element_type=jnp.float32)
            )
    return jnp.stack(taps).reshape(3, 3, padded.shape[0], grad_round.shape[0])


def per_device(ocean_field, cotangent, conv_weight, conv_bias, projection, mode_weight):
    chans, rows_dev, cols_dev = ocean_field.shape
    n_row = lax.axis_size("row")
    n_col = lax.axis_size("col")
    ky_dev = mode_weight.shape[0]
    kx_dev = mode_weight.shape[4]
    modes = ky_dev * n_row
    kx_all = kx_dev * n_col
    nx_all = rows_dev * n_row
    ny_all = cols_dev * n_col
    strip_rows = rows_dev // n_col
    row_at = lax.axis_index("row")
    col_at = lax.axis_index("col")
    scale = 1.0 / math.sqrt(nx_all * ny_all)
    my_cols = col_at * cols_dev + jnp.arange(cols_dev, dtype=jnp.int32)
    my_ky = row_at * ky_dev + jnp.arange(ky_dev, dtype=jnp.int32)
    kx_every = jnp.arange(kx_all, dtype=jnp.int32)
    set_rows = (
        jnp.arange(n_row, dtype=jnp.int32)[:, None] * rows_dev
        + col_at * strip_rows
        + jnp.arange(strip_rows, dtype=jnp.int32)[None, :]
    ).reshape(-1)
    ky_weight = jnp.where(jnp.arange(modes) == 0, 1.0, 2.0).astype(jnp.float32)
    mine_weight = jnp.where(my_ky == 0, 1.0, 2.0).astype(jnp.float32)

    def column_sums(field):
        partial_value = column_section(field, my_cols, modes, ny_all)
        return lax.psum_scatter(partial_value, "col", scatter_dimension=3, tiled=True)

    def forward_modes(field):
        whole_y = column_sums(field)
        by_ky = row_section(
            lax.all_to_all(whole_y, "row", split_axis=0, concat_axis=3, tiled=True),
            set_rows,
            kx_every,
            modes,
            nx_all,
        )
        return lax.psum_scatter(by_ky, "col", scatter_dimension=3, tiled=True)

    def to_grid(spectral, weights_ky):
        pieces = lax.all_gather(spectral, "col", axis=3, tiled=True)
        kx_ids = jnp.arange(pieces.shape[3], dtype=jnp.int32)
        summed = row_inverse(pieces, set_rows, kx_ids, modes, nx_all)
        returned = lax.all_to_all(summed, "row", split_axis=3, concat_axis=0, tiled=True)
        return column_inverse(
            lax.all_gather(returned, "col", axis=3, tiled=True),
            weights_ky,
            my_cols,
            modes,
            ny_all,
            scale,
        )

    padded_in = with_halo(ocean_field, (("row", 1), ("col", 2)), 1)
    spectrum = forward_modes(ocean_field) * scale
    mixed = mix_modes(spectrum, mode_weight).astype(jnp.bfloat16)
    spectral_cells = to_grid(mixed, ky_weight)
    pre_act = (
        conv_cells(padded_in, conv_weight, rows_dev, cols_dev)
        + spectral_cells
        + conv_bias[:, None, None]
    )
    activ, slope = gelu_parts(pre_act)
    cot_rows = cotangent.astype(jnp.float32)
    grad_pre = projection[:, None, None] * cot_rows[None] * slope
    grad_round = grad_pre.astype(jnp.bfloat16)
    kernel_part = kernel_grad(padded_in, grad_round, rows_dev, cols_dev)
    bias_part = jnp.sum(grad_pre, axis=(1, 2))
    proj_part = jnp.sum(activ * cot_rows[None], axis=(1, 2))
    kernel_sum, bias_sum, proj_sum = lax.psum((kernel_part, bias_part, proj_part), ("row", "col"))
    grad_modes = forward_modes(grad_round) * (scale * mine_weight)[:, None, None, None]
    grad_spec, grad_spectrum = mix_back(spectrum, mode_weight, grad_modes)
    padded_grad = with_halo(grad_round, (("row", 1), ("col", 2)), 1)
    back_cells = conv_transpose(padded_grad, conv_weight, rows_dev, cols_dev)
    spectral_back = to_grid(grad_spectrum, jnp.ones((modes,), jnp.float32))
    grad_input = back_cells + spectral_back
    return (grad_input, grad_spec, kernel_sum * scale, bias_sum * scale, proj_sum * scale)


def solution(mesh):
    placed = (
        P(None, "row", "col"),
        P("row", "col"),
        P(),
        P(),
        P(),
        P("row", None, None, None, "col"),
    )
    return jax.shard_map(
        per_device,
        mesh=mesh,
        in_specs=placed,
        out_specs=(P(None, "row", "col"), P("row", None, None, None, "col"), P(), P(), P()),
        check_vma=False,
    )
```

profile of v0, /device:TPU:2, one launch (start us, length us, event | category | flops | bytes accessed | tf_op | source)
XLA Modules:
  0.0 568.2 jit_solution(2146350703683208612)
XLA Ops:
  8.2 3.0 fusion.69
  11.3 58.2 %reduce-scatter.9.cloned.1.call-done = f32[128,2,32,8]{0,3,2,1:T(8,128)} async-done(((f32[128,2,32,64]{0,3,2,1:T(8,128)}), f32[128,2,32,8]{0,3,2,1:T(8,128)}) %reduce-scatter.9.cloned.1.call-update) | async-done | bytes 262160 | tf_op jit(solution)/shard_map/reduce_scatter | solution.py:170
  72.1 9.2 %all-to-all-start = ((f32[32,1,2048]{2,1,0:T(1,128)}), f32[32,1,2048]{2,1,0:T(1,128)S(1)}, u32[]{:S(2)}, u32[]{:S(2)}) async-start(f32[32,1,2048]{2,1,0:T(1,128)} %reshape.249), calls=%async_computation.1 | async-start | bytes 524288 | tf_op jit(solution)/shard_map/all_to_all | solution.py:175
  81.6 11.0 %all-to-all-done = f32[32,1,2048]{2,1,0:T(1,128)S(1)} async-done(((f32[32,1,2048]{2,1,0:T(1,128)}), f32[32,1,2048]{2,1,0:T(1,128)S(1)}, u32[]{:S(2)}, u32[]{:S(2)}) %all-to-all-start) | async-done | bytes 262176 | tf_op jit(solution)/shard_map/all_to_all | solution.py:175
  100.9 1.9 reshape.245
  102.8 35.6 %reduce-scatter.13.cloned.1.call-done = f32[32,256]{1,0:T(8,128)} async-done(((f32[256,256]{1,0:T(8,128)}), f32[32,256]{1,0:T(8,128)}) %reduce-scatter.13.cloned.1.call-update) | async-done | bytes 32784
  141.6 30.2 %all_gather.12 = bf16[4,2,32,256]{2,0,1,3:T(4,128)(2,1)S(1)} all-gather(bf16[4,2,32,32]{2,0,1,3:T(4,128)(2,1)S(1)} %pad_maximum_fusion.14), channel_id=1, replica_groups=mesh['row'=32,'col'=8] {'col'}, dimensions={3}, use_global_device_ids=true | all-gather | bytes 147456 | tf_op jit(solution)/shard_map/all_gather | solution.py:184
  176.4 19.8 %all_to_all.72 = f32[32,1,2048]{2,1,0:T(1,128)S(1)} all-to-all(f32[32,1,2048]{2,1,0:T(1,128)S(1)} %reshape.251), channel_id=1, replica_groups=mesh['row'=32,'col'=8] {'row'}, dimensions={0} | all-to-all | bytes 524288 | tf_op jit(solution)/shard_map/all_to_all | solution.py:187
  200.0 3.9 collective-permute-start.1
  204.0 1.9 collective-permute-start
  205.9 2.1 fusion.120
  217.4 3.0 fusion.55
  220.4 3.0 fusion.57
  226.1 1.9 fusion.76
  228.0 1.9 fusion.131
  229.8 1.9 fusion.123
  231.7 2.0 fusion.126
  233.8 2.0 fusion.116
  235.8 13.8 %all-gather.3.cloned.1.call-done = f32[128,2,32,64]{0,3,2,1:T(8,128)} async-done(((f32[128,2,32,8]{0,3,2,1:T(8,128)}), f32[128,2,32,64]{0,3,2,1:T(8,128)}) %all-gather.3.cloned.1.call-update) | async-done | bytes 2097168 | tf_op jit(solution)/shard_map/all_gather | solution.py:189
  249.6 1.9 broadcast_multiply_fusion
  251.6 2.5 fusion.16
  254.2 6.1 %multiply_reduce_fusion = (f32[32]{0:T(128)}, f32[32]{0:T(128)}, f32[32,64,256]{2,0,1:T(8,128)S(1)}, f32[32,64,256]{2,0,1:T(8,128)S(1)}) fusion(f32[64,256]{1,0:T(8,128)S(1)} %convert_element_type.77, f32[32]{0:T(128)S(1)} %copy-done.26, f32[32]{0:T(128)S(1)} %copy-done.29, f32[32,64,256,1]{2,0,3,1:T(8,128)S(1)} %fusion.16, ...), kind=kOutput, calls=%fused_computation.37 | convolution fusion | flops 48758720 | bytes 24765696 | tf_op jit(solution)/shard_map/io,ixy->oxy/dot_general | solution.py:113
  261.0 2.6 fusion.63
  264.2 1.9 collective-permute-start.5
  266.2 2.7 collective-permute-start.4
  268.9 2.2 fusion.28
  274.6 44.0 %reduce-scatter.11.cloned.1.call-done = f32[128,2,32,8]{0,3,2,1:T(8,128)} async-done(((f32[128,2,32,64]{0,3,2,1:T(8,128)}), f32[128,2,32,8]{0,3,2,1:T(8,128)}) %reduce-scatter.11.cloned.1.call-update) | async-done | bytes 262160 | tf_op jit(solution)/shard_map/reduce_scatter | solution.py:170
  318.5 2.3 copy.252
  320.9 2.4 reshape.253
  323.2 9.3 %all-to-all-start.2 = ((f32[32,1,2048]{2,1,0:T(1,128)}), f32[32,1,2048]{2,1,0:T(1,128)}, u32[]{:S(2)}, u32[]{:S(2)}) async-start(f32[32,1,2048]{2,1,0:T(1,128)} %reshape.253), calls=%async_computation.4 | async-start | bytes 524288 | tf_op jit(solution)/shard_map/all_to_all | solution.py:175
  336.5 7.3 %all-to-all-done.2 = f32[32,1,2048]{2,1,0:T(1,128)} async-done(((f32[32,1,2048]{2,1,0:T(1,128)}), f32[32,1,2048]{2,1,0:T(1,128)}, u32[]{:S(2)}, u32[]{:S(2)}) %all-to-all-start.2) | async-done | bytes 262176 | tf_op jit(solution)/shard_map/all_to_all | solution.py:175
  343.8 2.9 reduce.18
  352.5 2.1 copy.366
  354.6 3.1 reshape.247
  360.1 76.0 %all-reduce = (f32[3,3,32,32]{3,2,1,0:T(8,128)}, f32[32]{0:T(128)S(1)}, f32[32]{0:T(128)S(1)}) all-reduce(f32[3,3,32,32]{3,2,1,0:T(8,128)} %bitcast.123, f32[32]{0:T(128)S(1)} %copy-done.28, f32[32]{0:T(128)S(1)} %copy-done.27), channel_id=1, replica_groups=mesh['row'=32,'col'=8] {'row','col'}, use_global_device_ids=true, to_apply=%region_4.5 | all-reduce | flops 9280 | bytes 74240 | tf_op jit(solution)/shard_map/psum | solution.py:213
  437.9 3.4 fusion.6
  441.8 30.0 %all_gather.14 = bf16[4,2,32,256]{2,0,1,3:T(4,128)(2,1)S(1)} all-gather(bf16[4,2,32,32]{2,0,1,3:T(4,128)(2,1)S(1)} %pad_maximum_fusion.15), channel_id=1, replica_groups=mesh['row'=32,'col'=8] {'col'}, dimensions={3}, use_global_device_ids=true | all-gather | bytes 147456 | tf_op jit(solution)/shard_map/all_gather | solution.py:184
  477.1 6.3 %all-to-all-start.3 = ((f32[32,1,2048]{2,1,0:T(1,128)}), f32[32,1,2048]{2,1,0:T(1,128)S(1)}, u32[]{:S(2)}, u32[]{:S(2)}) async-start(f32[32,1,2048]{2,1,0:T(1,128)} %reshape.255), calls=%async_computation.5 | async-start | bytes 524288 | tf_op jit(solution)/shard_map/all_to_all | solution.py:187
  485.9 8.4 %all-to-all-done.3 = f32[32,1,2048]{2,1,0:T(1,128)S(1)} async-done(((f32[32,1,2048]{2,1,0:T(1,128)}), f32[32,1,2048]{2,1,0:T(1,128)S(1)}, u32[]{:S(2)}, u32[]{:S(2)}) %all-to-all-start.3) | async-done | bytes 262176 | tf_op jit(solution)/shard_map/all_to_all | solution.py:187
  503.2 4.5 collective-permute-start.7
  507.7 2.5 fusion.33
  514.6 2.3 maximum_maximum_fusion
  520.4 1.9 fusion.45
  526.6 2.9 pad_maximum_fusion
  529.5 18.4 %all-gather.5.cloned.1.call-done = f32[128,2,32,64]{0,3,1,2:T(8,128)} async-done(((f32[128,2,32,8]{0,3,1,2:T(8,128)}), f32[128,2,32,64]{0,3,1,2:T(8,128)}) %all-gather.5.cloned.1.call-update) | async-done | bytes 2097168 | tf_op jit(solution)/shard_map/all_gather | solution.py:189
  547.9 4.2 fusion.18
  552.1 6.3 %fusion.13 = f32[32,64,256]{2,0,1:T(8,128)S(1)} fusion(f32[32,64,256,1]{2,0,3,1:T(8,128)S(1)} %fusion.18, f32[64,256,32]{1,2,0:T(8,128)S(1)} %copy-done.12, f32[64,256,32]{1,2,0:T(8,128)} %fusion.45, f32[64,256,32]{1,2,0:T(8,128)} %fusion.47, f32[64,256,32]{1,2,0:T(8,128)S(1)} %copy-done.11, f32[64,256,32]{1,2,0:T(8,128)} %fusion.49, ...), kind=kOutput, calls=%fused_computation.24 | convolution fusion | flops 38797312 | bytes 22028288 | tf_op jit(solution)/shard_map/io,oxy->ixy/dot_general | solution.py:126
  558.4 2.5 copy.265
  (192 shorter events, 83.5 us)
Async XLA Ops:
  7.2 62.3 %reduce-scatter.9.cloned.1.call-start = ((), (), s32[]{:S(2)}) async-start(), calls=%async_computation.8 | async-start | bytes 2359296 | tf_op jit(solution)/shard_map/reduce_scatter | solution.py:170
  72.1 20.4 %all-to-all-start = ((f32[32,1,2048]{2,1,0:T(1,128)}), f32[32,1,2048]{2,1,0:T(1,128)S(1)}, u32[]{:S(2)}, u32[]{:S(2)}) async-start(f32[32,1,2048]{2,1,0:T(1,128)} %reshape.249), calls=%async_computation.1 | async-start | bytes 524288 | tf_op jit(solution)/shard_map/all_to_all | solution.py:175
  81.3 57.1 %reduce-scatter.13.cloned.1.call-start = ((), (), s32[]{:S(2)}) async-start(), calls=%async_computation.12 | async-start | bytes 294912
  99.1 41.0 %copy-start.13 = (bf16[4,2,32,32,32]{4,3,2,1,0:T(8,128)(2,1)S(1)}, bf16[4,2,32,32,32]{4,3,2,1,0:T(8,128)(2,1)}, u32[]{:S(2)}) copy-start(bf16[4,2,32,32,32]{4,3,2,1,0:T(8,128)(2,1)} %param.11) | copy-start | bytes 1572868
  102.8 146.8 %all-gather.3.cloned.1.call-start = ((), (), s32[]{:S(2)}) async-start(), calls=%async_computation.9 | async-start | bytes 2359296 | tf_op jit(solution)/shard_map/all_gather | solution.py:189
  198.6 1.4 copy-start
  198.6 7.3 %copy-start.19 = (bf16[3,3,32,32]{3,2,1,0:T(8,128)(2,1)S(1)}, bf16[3,3,32,32]{3,2,1,0:T(8,128)(2,1)}, u32[]{:S(2)}) copy-start(bf16[3,3,32,32]{3,2,1,0:T(8,128)(2,1)} %param.8) | copy-start | bytes 55300
  199.9 8.1 %copy-start.25 = (bf16[64,256]{1,0:T(8,128)(2,1)S(1)}, bf16[64,256]{1,0:T(8,128)(2,1)}, u32[]{:S(2)}) copy-start(bf16[64,256]{1,0:T(8,128)(2,1)} %param.7) | copy-start | bytes 98308
  199.9 118.6 %reduce-scatter.11.cloned.1.call-start = ((), (), s32[]{:S(2)}) async-start(), calls=%async_computation.10 | async-start | bytes 2359296 | tf_op jit(solution)/shard_map/reduce_scatter | solution.py:170
  200.0 9.7 %collective-permute-start.1 = (bf16[32,1,256]{2,0,1:T(8,128)(2,1)S(1)}, bf16[32,1,256]{2,0,1:T(8,128)(2,1)S(1)}, u32[]{:S(2)}, u32[]{:S(2)}) collective-permute-start(bf16[32,1,256]{2,0,1:T(8,128)(2,1)S(1)} %copy.414), channel_id=1, source_target_pairs={{8,0},{16,8},{24,16},{32,24},{40,32},{48,40},{56,48},{64,56},{72,6... | collective-permute-start | bytes 49160 | tf_op jit(solution)/shard_map/ppermute | solution.py:19
  204.0 5.1 collective-permute-start
  209.7 1.3 copy-start.17
  209.7 1.1 copy-start.1
  214.4 10.7 %collective-permute-start.2 = (bf16[32,66,1]{1,0,2:T(8,128)(2,1)S(1)}, bf16[32,66,1]{1,0,2:T(8,128)(2,1)S(1)}, u32[]{:S(2)}, u32[]{:S(2)}) collective-permute-start(bf16[32,66,1]{1,0,2:T(8,128)(2,1)S(1)} %copy.210), channel_id=1, source_target_pairs={{0,1},{1,2},{2,3},{3,4},{4,5},{5,6},{6,7},{8,9},{9,10},{10,11},{11... | collective-permute-start | bytes 12680 | tf_op jit(solution)/shard_map/ppermute | solution.py:18
  215.7 7.7 %collective-permute-start.3 = (bf16[32,66,1]{1,0,2:T(8,128)(2,1)S(1)}, bf16[32,66,1]{1,0,2:T(8,128)(2,1)S(1)}, u32[]{:S(2)}, u32[]{:S(2)}) collective-permute-start(bf16[32,66,1]{1,0,2:T(8,128)(2,1)S(1)} %copy.215), channel_id=1, source_target_pairs={{1,0},{2,1},{3,2},{4,3},{5,4},{6,5},{7,6},{9,8},{10,9},{11,10},{12... | collective-permute-start | bytes 12680 | tf_op jit(solution)/shard_map/ppermute | solution.py:19
  226.1 3.7 copy-start.3
  229.8 1.9 copy-start.6
  249.6 4.5 copy-start.15
  249.6 4.5 copy-start.16
  251.6 2.6 copy-start.7
  251.6 2.6 copy-start.14
  251.6 2.6 copy-start.26
  251.6 2.6 copy-start.29
  263.6 7.5 %copy-start.18 = (bf16[32,65,256]{2,0,1:T(8,128)(2,1)S(1)}, bf16[32,65,256]{2,0,1:T(8,128)(2,1)}, u32[]{:S(2)}) copy-start(bf16[32,65,256]{2,0,1:T(8,128)(2,1)} %copy-done.17) | copy-start | bytes 3194884
  264.2 234.9 %collective-permute-start.5 = (bf16[32,1,256]{2,0,1:T(8,128)(2,1)}, bf16[32,1,256]{2,0,1:T(8,128)(2,1)S(1)}, u32[]{:S(2)}, u32[]{:S(2)}) collective-permute-start(bf16[32,1,256]{2,0,1:T(8,128)(2,1)} %get-tuple-element.54), channel_id=1, source_target_pairs={{8,0},{16,8},{24,16},{32,24},{40,32},{48,40},{56,48},{64,56},{72,6... | collective-permute-start | bytes 49160 | tf_op jit(solution)/shard_map/ppermute | solution.py:19
  266.2 6.0 %copy-start.8 = (bf16[32,66,1]{2,0,1:T(8,128)(2,1)S(1)}, bf16[32,66,1]{2,0,1:T(8,128)(2,1)}, u32[]{:S(2)}) copy-start(bf16[32,66,1]{2,0,1:T(8,128)(2,1)} %copy.216) | copy-start | bytes 12676
  266.2 233.0 %collective-permute-start.4 = (bf16[32,1,256]{2,0,1:T(8,128)(2,1)}, bf16[32,1,256]{2,0,1:T(8,128)(2,1)}, u32[]{:S(2)}, u32[]{:S(2)}) collective-permute-start(bf16[32,1,256]{2,0,1:T(8,128)(2,1)} %get-tuple-element.55), channel_id=1, source_target_pairs={{0,8},{8,16},{16,24},{24,32},{32,40},{40,48},{48,56},{56,64},{64,7... | collective-permute-start | bytes 49160 | tf_op jit(solution)/shard_map/ppermute | solution.py:18
  272.1 1.3 copy-start.4
  323.2 20.6 %all-to-all-start.2 = ((f32[32,1,2048]{2,1,0:T(1,128)}), f32[32,1,2048]{2,1,0:T(1,128)}, u32[]{:S(2)}, u32[]{:S(2)}) async-start(f32[32,1,2048]{2,1,0:T(1,128)} %reshape.253), calls=%async_computation.4 | async-start | bytes 524288 | tf_op jit(solution)/shard_map/all_to_all | solution.py:175
  332.6 103.6 %reduce-scatter.15.cloned.1.call-start = ((), (), s32[]{:S(2)}) async-start(), calls=%async_computation.13 | async-start | bytes 294912
  332.6 1.4 copy-start.9
  334.0 1.3 copy-start.5
  351.7 6.1 %copy-start.2 = (bf16[32,65,256]{2,0,1:T(8,128)(2,1)S(1)}, bf16[32,65,256]{2,0,1:T(8,128)(2,1)}, u32[]{:S(2)}) copy-start(bf16[32,65,256]{2,0,1:T(8,128)(2,1)} %copy-done.1) | copy-start | bytes 3194884
  357.8 1.1 copy-start.10
  357.8 2.4 copy-start.27
  357.8 2.3 copy-start.28
  474.6 8.9 %copy-start.24 = (f32[3,3,32,32]{3,2,1,0:T(8,128)S(1)}, f32[3,3,32,32]{3,2,1,0:T(8,128)}, u32[]{:S(2)}) copy-start(f32[3,3,32,32]{3,2,1,0:T(8,128)} %get-tuple-element.44) | copy-start | bytes 110596
  477.1 17.2 %all-to-all-start.3 = ((f32[32,1,2048]{2,1,0:T(1,128)}), f32[32,1,2048]{2,1,0:T(1,128)S(1)}, u32[]{:S(2)}, u32[]{:S(2)}) async-start(f32[32,1,2048]{2,1,0:T(1,128)} %reshape.255), calls=%async_computation.5 | async-start | bytes 524288 | tf_op jit(solution)/shard_map/all_to_all | solution.py:187
  483.4 64.4 %all-gather.5.cloned.1.call-start = ((), (), s32[]{:S(2)}) async-start(), calls=%async_computation.11 | async-start | bytes 2359296 | tf_op jit(solution)/shard_map/all_gather | solution.py:189
  499.1 11.0 %copy-start.23 = (bf16[32,1,256]{2,0,1:T(8,128)(2,1)}, bf16[32,1,256]{2,0,1:T(8,128)(2,1)S(1)}, u32[]{:S(2)}) copy-start(bf16[32,1,256]{2,0,1:T(8,128)(2,1)S(1)} %collective-permute-done.5) | copy-start | bytes 49156
  501.6 11.3 %collective-permute-start.6 = (bf16[32,66,1]{1,0,2:T(8,128)(2,1)S(1)}, bf16[32,66,1]{1,0,2:T(8,128)(2,1)S(1)}, u32[]{:S(2)}, u32[]{:S(2)}) collective-permute-start(bf16[32,66,1]{1,0,2:T(8,128)(2,1)S(1)} %copy.238), channel_id=1, source_target_pairs={{1,0},{2,1},{3,2},{4,3},{5,4},{6,5},{7,6},{9,8},{10,9},{11,10},{12... | collective-permute-start | bytes 12680 | tf_op jit(solution)/shard_map/ppermute | solution.py:19
  503.2 8.8 %collective-permute-start.7 = (bf16[32,66,1]{1,0,2:T(8,128)(2,1)S(1)}, bf16[32,66,1]{1,0,2:T(8,128)(2,1)S(1)}, u32[]{:S(2)}, u32[]{:S(2)}) collective-permute-start(bf16[32,66,1]{1,0,2:T(8,128)(2,1)S(1)} %copy.242), channel_id=1, source_target_pairs={{0,1},{1,2},{2,3},{3,4},{4,5},{5,6},{6,7},{8,9},{9,10},{10,11},{11... | collective-permute-start | bytes 12680 | tf_op jit(solution)/shard_map/ppermute | solution.py:18
  524.1 1.8 copy-start.20
  524.1 1.8 copy-start.21
  524.1 1.8 copy-start.22
  547.9 4.2 copy-start.11
  547.9 4.2 copy-start.12
Sparse Core Ops, SparseCore 0:
  11.4 58.0 reduce-scatter.8
  102.9 35.4 reduce-scatter.12
  200.0 49.5 all-gather.2
  263.7 54.7 reduce-scatter.10
  357.9 35.5 reduce-scatter.14
  498.2 49.6 all-gather.4
where the time goes:
time: 577 us; the launch traced here: 568 us
  waiting for transfers between devices  198 us (34%)
  blocking collectives  156 us (27%)
  matrix products  81.5 us (14%)
  local copies, waits for them, and re-layouts  47.8 us (8%)
  starting transfers between devices  44.6 us (8%)
  other arithmetic  25.1 us (4%)
  between operations  15.4 us (3%)
    reduce_scatter x2, waiting for transfers between devices, column_sums(): lax.psum_scatter(partial_value, 'col', scatter_dimension=3, tiled=True)  102 us
    psum x1, blocking collectives, per_device(): lax.psum((kernel_part, bias_part, proj_part), ('row', 'col'))  76 us
    all_gather x2, blocking collectives, to_grid(): pieces = lax.all_gather(spectral, 'col', axis=3, tiled=True)  60.2 us
    unnamed x8, waiting for transfers between devices  35.7 us
    all_gather x2, waiting for transfers between devices, to_grid(): lax.all_gather(returned, 'col', axis=3, tiled=True)  32.3 us
    unnamed x80, local copies, waits for them, and re-layouts  24.7 us
    dot_general x9, matrix products, conv_cells(): jnp.einsum('io,ixy->oxy', kernel[tap_row, tap_col], shifted, preferred_el...  23.9 us
    dot_general x9, matrix products, conv_transpose(): jnp.einsum('io,oxy->ixy', kernel[tap_row, tap_col], shifted, preferred_el...  21.3 us
  transfers between devices with their start and end apart: 17, of which 9 were waited for; matrix products, arithmetic and copies ran while one was open for 17% of the time, Pallas kernels for 0%

commit v1 on v0

--- a/solution.py
+++ b/solution.py
@@ -210,7 +210,9 @@
     kernel_part = kernel_grad(padded_in, grad_round, rows_dev, cols_dev)
     bias_part = jnp.sum(grad_pre, axis=(1, 2))
     proj_part = jnp.sum(activ * cot_rows[None], axis=(1, 2))
-    kernel_sum, bias_sum, proj_sum = lax.psum((kernel_part, bias_part, proj_part), ("row", "col"))
+    kernel_sum, bias_sum, proj_sum = lax.psum(
+        lax.psum((kernel_part, bias_part, proj_part), "col"), "row"
+    )
     grad_modes = forward_modes(grad_round) * (scale * mine_weight)[:, None, None, None]
     grad_spec, grad_spectrum = mix_back(spectrum, mode_weight, grad_modes)
     padded_grad = with_halo(grad_round, (("row", 1), ("col", 2)), 1)

time: 577 us -> 677 us (1.17)
  blocking collectives: 156 us -> 251 us
    psum x1 -> x2, blocking collectives: 76 us -> 172 us  [the longest x1 136 us: per_device(): lax.psum(lax.psum((kernel_part, bias_part, proj_part), 'col'), 'row')]
  transfers between devices with their start and end apart: 17 -> 17, of which waited for: 9 -> 9; matrix products, arithmetic and copies ran while one was open for 17% -> 15% of each run, Pallas kernels for 0% -> 0%
where the time goes in v1:
time: 677 us; the launch traced here: 668 us
  blocking collectives  251 us (37%)
  waiting for transfers between devices  198 us (29%)
  matrix products  81.4 us (12%)
  starting transfers between devices  48.8 us (7%)
  local copies, waits for them, and re-layouts  47.7 us (7%)
  other arithmetic  25.1 us (4%)
  between operations  15.4 us (2%)
    psum x1, blocking collectives, per_device(): lax.psum(lax.psum((kernel_part, bias_part, proj_part), 'col'), 'row')  136 us
    reduce_scatter x2, waiting for transfers between devices, column_sums(): lax.psum_scatter(partial_value, 'col', scatter_dimension=3, tiled=True)  102 us
    all_gather x2, blocking collectives, to_grid(): pieces = lax.all_gather(spectral, 'col', axis=3, tiled=True)  59.7 us
    psum x1, blocking collectives, per_device(): lax.psum((kernel_part, bias_part, proj_part), 'col')  36.1 us
    unnamed x8, waiting for transfers between devices  35.7 us
    all_gather x2, waiting for transfers between devices, to_grid(): lax.all_gather(returned, 'col', axis=3, tiled=True)  32.5 us
    unnamed x80, local copies, waits for them, and re-layouts  24.6 us
    dot_general x9, matrix products, conv_cells(): jnp.einsum('io,ixy->oxy', kernel[tap_row, tap_col], shifted, preferred_el...  23.8 us
  transfers between devices with their start and end apart: 17, of which 9 were waited for; matrix products, arithmetic and copies ran while one was open for 15% of the time, Pallas kernels for 0%

profile of v1, /device:TPU:2, one launch (start us, length us, event | category | flops | bytes accessed | tf_op | source)
XLA Modules:
  0.0 667.9 jit_solution(13016569774902437675)
XLA Ops:
  8.2 3.0 fusion.69
  11.3 58.2 %reduce-scatter.9.cloned.1.call-done = f32[128,2,32,8]{0,3,2,1:T(8,128)} async-done(((f32[128,2,32,64]{0,3,2,1:T(8,128)}), f32[128,2,32,8]{0,3,2,1:T(8,128)}) %reduce-scatter.9.cloned.1.call-update) | async-done | bytes 262160 | tf_op jit(solution)/shard_map/reduce_scatter | solution.py:170
  72.1 9.2 %all-to-all-start = ((f32[32,1,2048]{2,1,0:T(1,128)}), f32[32,1,2048]{2,1,0:T(1,128)S(1)}, u32[]{:S(2)}, u32[]{:S(2)}) async-start(f32[32,1,2048]{2,1,0:T(1,128)} %reshape.249), calls=%async_computation.1 | async-start | bytes 524288 | tf_op jit(solution)/shard_map/all_to_all | solution.py:175
  81.6 11.0 %all-to-all-done = f32[32,1,2048]{2,1,0:T(1,128)S(1)} async-done(((f32[32,1,2048]{2,1,0:T(1,128)}), f32[32,1,2048]{2,1,0:T(1,128)S(1)}, u32[]{:S(2)}, u32[]{:S(2)}) %all-to-all-start) | async-done | bytes 262176 | tf_op jit(solution)/shard_map/all_to_all | solution.py:175
  100.9 1.9 reshape.245
  102.8 35.6 %reduce-scatter.13.cloned.1.call-done = f32[32,256]{1,0:T(8,128)} async-done(((f32[256,256]{1,0:T(8,128)}), f32[32,256]{1,0:T(8,128)}) %reduce-scatter.13.cloned.1.call-update) | async-done | bytes 32784
  141.6 30.2 %all_gather.12 = bf16[4,2,32,256]{2,0,1,3:T(4,128)(2,1)S(1)} all-gather(bf16[4,2,32,32]{2,0,1,3:T(4,128)(2,1)S(1)} %pad_maximum_fusion.14), channel_id=1, replica_groups=mesh['row'=32,'col'=8] {'col'}, dimensions={3}, use_global_device_ids=true | all-gather | bytes 147456 | tf_op jit(solution)/shard_map/all_gather | solution.py:184
  176.4 19.8 %all_to_all.72 = f32[32,1,2048]{2,1,0:T(1,128)S(1)} all-to-all(f32[32,1,2048]{2,1,0:T(1,128)S(1)} %reshape.251), channel_id=1, replica_groups=mesh['row'=32,'col'=8] {'row'}, dimensions={0} | all-to-all | bytes 524288 | tf_op jit(solution)/shard_map/all_to_all | solution.py:187
  200.0 3.9 collective-permute-start.1
  204.0 1.9 collective-permute-start
  205.9 2.1 fusion.120
  217.4 3.0 fusion.55
  220.4 3.0 fusion.57
  228.0 1.9 fusion.131
  229.8 1.9 fusion.123
  231.7 2.0 fusion.126
  233.8 2.0 fusion.116
  235.8 13.8 %all-gather.3.cloned.1.call-done = f32[128,2,32,64]{0,3,2,1:T(8,128)} async-done(((f32[128,2,32,8]{0,3,2,1:T(8,128)}), f32[128,2,32,64]{0,3,2,1:T(8,128)}) %all-gather.3.cloned.1.call-update) | async-done | bytes 2097168 | tf_op jit(solution)/shard_map/all_gather | solution.py:189
  249.6 1.9 broadcast_multiply_fusion
  251.6 2.5 fusion.16
  254.1 6.1 multiply_reduce_fusion
  260.9 2.6 fusion.63
  264.2 1.9 collective-permute-start.5
  266.1 2.7 collective-permute-start.4
  268.8 2.2 fusion.28
  274.5 44.0 %reduce-scatter.11.cloned.1.call-done = f32[128,2,32,8]{0,3,2,1:T(8,128)} async-done(((f32[128,2,32,64]{0,3,2,1:T(8,128)}), f32[128,2,32,8]{0,3,2,1:T(8,128)}) %reduce-scatter.11.cloned.1.call-update) | async-done | bytes 262160 | tf_op jit(solution)/shard_map/reduce_scatter | solution.py:170
  318.6 2.3 copy.252
  320.9 2.4 reshape.253
  323.3 9.3 %all-to-all-start.2 = ((f32[32,1,2048]{2,1,0:T(1,128)}), f32[32,1,2048]{2,1,0:T(1,128)}, u32[]{:S(2)}, u32[]{:S(2)}) async-start(f32[32,1,2048]{2,1,0:T(1,128)} %reshape.253), calls=%async_computation.4 | async-start | bytes 524288 | tf_op jit(solution)/shard_map/all_to_all | solution.py:175
  336.6 7.3 %all-to-all-done.2 = f32[32,1,2048]{2,1,0:T(1,128)} async-done(((f32[32,1,2048]{2,1,0:T(1,128)}), f32[32,1,2048]{2,1,0:T(1,128)}, u32[]{:S(2)}, u32[]{:S(2)}) %all-to-all-start.2) | async-done | bytes 262176 | tf_op jit(solution)/shard_map/all_to_all | solution.py:175
  343.8 2.9 reduce.18
  352.5 2.1 copy.366
  354.6 3.1 reshape.247
  360.1 36.1 %all-reduce.1 = (f32[3,3,32,32]{3,2,1,0:T(8,128)S(1)}, f32[32]{0:T(128)S(1)}, f32[32]{0:T(128)S(1)}) all-reduce(f32[3,3,32,32]{3,2,1,0:T(8,128)} %bitcast.123, f32[32]{0:T(128)S(1)} %copy-done.28, f32[32]{0:T(128)S(1)} %copy-done.27), channel_id=1, replica_groups=mesh['row'=32,'col'=8] {'col'}, use_global_device_ids=true, to_apply=%region_4.5 | all-reduce | flops 9280 | bytes 74240 | tf_op jit(solution)/shard_map/psum | solution.py:214
  396.2 135.8 %all-reduce = (f32[3,3,32,32]{3,2,1,0:T(8,128)}, f32[32]{0:T(128)S(1)}, f32[32]{0:T(128)S(1)}) all-reduce(f32[3,3,32,32]{3,2,1,0:T(8,128)S(1)} %get-tuple-element.47, f32[32]{0:T(128)S(1)} %get-tuple-element.48, f32[32]{0:T(128)S(1)} %get-tuple-element.49), channel_id=1, replica_groups=mesh['row'=32,'col'=8] {'row'}, use_global_device_ids=true, to_apply=%region_5.6 | all-reduce | flops 9280 | bytes 74240 | tf_op jit(solution)/shard_map/psum | solution.py:213
  533.8 3.4 fusion.6
  537.7 29.5 %all_gather.14 = bf16[4,2,32,256]{2,0,1,3:T(4,128)(2,1)S(1)} all-gather(bf16[4,2,32,32]{2,0,1,3:T(4,128)(2,1)S(1)} %pad_maximum_fusion.15), channel_id=1, replica_groups=mesh['row'=32,'col'=8] {'col'}, dimensions={3}, use_global_device_ids=true | all-gather | bytes 147456 | tf_op jit(solution)/shard_map/all_gather | solution.py:184
  572.6 10.5 %all-to-all-start.3 = ((f32[32,1,2048]{2,1,0:T(1,128)}), f32[32,1,2048]{2,1,0:T(1,128)S(1)}, u32[]{:S(2)}, u32[]{:S(2)}) async-start(f32[32,1,2048]{2,1,0:T(1,128)} %reshape.255), calls=%async_computation.5 | async-start | bytes 524288 | tf_op jit(solution)/shard_map/all_to_all | solution.py:187
  585.5 8.3 %all-to-all-done.3 = f32[32,1,2048]{2,1,0:T(1,128)S(1)} async-done(((f32[32,1,2048]{2,1,0:T(1,128)}), f32[32,1,2048]{2,1,0:T(1,128)S(1)}, u32[]{:S(2)}, u32[]{:S(2)}) %all-to-all-start.3) | async-done | bytes 262176 | tf_op jit(solution)/shard_map/all_to_all | solution.py:187
  602.4 4.8 collective-permute-start.7
  607.2 2.5 fusion.33
  614.1 2.3 maximum_maximum_fusion
  619.9 1.9 fusion.45
  626.1 2.9 pad_maximum_fusion
  628.9 18.7 %all-gather.5.cloned.1.call-done = f32[128,2,32,64]{0,3,1,2:T(8,128)} async-done(((f32[128,2,32,8]{0,3,1,2:T(8,128)}), f32[128,2,32,64]{0,3,1,2:T(8,128)}) %all-gather.5.cloned.1.call-update) | async-done | bytes 2097168 | tf_op jit(solution)/shard_map/all_gather | solution.py:189
  647.6 4.2 fusion.18
  651.8 6.3 fusion.13
  658.1 2.5 copy.265
  (193 shorter events, 85.1 us)
Async XLA Ops:
  7.2 62.3 %reduce-scatter.9.cloned.1.call-start = ((), (), s32[]{:S(2)}) async-start(), calls=%async_computation.8 | async-start | bytes 2359296 | tf_op jit(solution)/shard_map/reduce_scatter | solution.py:170
  72.1 20.4 %all-to-all-start = ((f32[32,1,2048]{2,1,0:T(1,128)}), f32[32,1,2048]{2,1,0:T(1,128)S(1)}, u32[]{:S(2)}, u32[]{:S(2)}) async-start(f32[32,1,2048]{2,1,0:T(1,128)} %reshape.249), calls=%async_computation.1 | async-start | bytes 524288 | tf_op jit(solution)/shard_map/all_to_all | solution.py:175
  81.3 57.1 %reduce-scatter.13.cloned.1.call-start = ((), (), s32[]{:S(2)}) async-start(), calls=%async_computation.12 | async-start | bytes 294912
  99.1 41.0 %copy-start.13 = (bf16[4,2,32,32,32]{4,3,2,1,0:T(8,128)(2,1)S(1)}, bf16[4,2,32,32,32]{4,3,2,1,0:T(8,128)(2,1)}, u32[]{:S(2)}) copy-start(bf16[4,2,32,32,32]{4,3,2,1,0:T(8,128)(2,1)} %param.11) | copy-start | bytes 1572868
  102.8 146.8 %all-gather.3.cloned.1.call-start = ((), (), s32[]{:S(2)}) async-start(), calls=%async_computation.9 | async-start | bytes 2359296 | tf_op jit(solution)/shard_map/all_gather | solution.py:189
  198.6 1.4 copy-start
  198.6 7.3 %copy-start.19 = (bf16[3,3,32,32]{3,2,1,0:T(8,128)(2,1)S(1)}, bf16[3,3,32,32]{3,2,1,0:T(8,128)(2,1)}, u32[]{:S(2)}) copy-start(bf16[3,3,32,32]{3,2,1,0:T(8,128)(2,1)} %param.8) | copy-start | bytes 55300
  199.9 8.1 %copy-start.25 = (bf16[64,256]{1,0:T(8,128)(2,1)S(1)}, bf16[64,256]{1,0:T(8,128)(2,1)}, u32[]{:S(2)}) copy-start(bf16[64,256]{1,0:T(8,128)(2,1)} %param.7) | copy-start | bytes 98308
  199.9 118.7 %reduce-scatter.11.cloned.1.call-start = ((), (), s32[]{:S(2)}) async-start(), calls=%async_computation.10 | async-start | bytes 2359296 | tf_op jit(solution)/shard_map/reduce_scatter | solution.py:170
  200.0 9.7 %collective-permute-start.1 = (bf16[32,1,256]{2,0,1:T(8,128)(2,1)S(1)}, bf16[32,1,256]{2,0,1:T(8,128)(2,1)S(1)}, u32[]{:S(2)}, u32[]{:S(2)}) collective-permute-start(bf16[32,1,256]{2,0,1:T(8,128)(2,1)S(1)} %copy.414), channel_id=1, source_target_pairs={{8,0},{16,8},{24,16},{32,24},{40,32},{48,40},{56,48},{64,56},{72,6... | collective-permute-start | bytes 49160 | tf_op jit(solution)/shard_map/ppermute | solution.py:19
  204.0 5.1 collective-permute-start
  209.7 1.3 copy-start.17
  209.7 1.0 copy-start.1
  214.4 10.7 %collective-permute-start.2 = (bf16[32,66,1]{1,0,2:T(8,128)(2,1)S(1)}, bf16[32,66,1]{1,0,2:T(8,128)(2,1)S(1)}, u32[]{:S(2)}, u32[]{:S(2)}) collective-permute-start(bf16[32,66,1]{1,0,2:T(8,128)(2,1)S(1)} %copy.210), channel_id=1, source_target_pairs={{0,1},{1,2},{2,3},{3,4},{4,5},{5,6},{6,7},{8,9},{9,10},{10,11},{11... | collective-permute-start | bytes 12680 | tf_op jit(solution)/shard_map/ppermute | solution.py:18
  215.7 7.7 %collective-permute-start.3 = (bf16[32,66,1]{1,0,2:T(8,128)(2,1)S(1)}, bf16[32,66,1]{1,0,2:T(8,128)(2,1)S(1)}, u32[]{:S(2)}, u32[]{:S(2)}) collective-permute-start(bf16[32,66,1]{1,0,2:T(8,128)(2,1)S(1)} %copy.215), channel_id=1, source_target_pairs={{1,0},{2,1},{3,2},{4,3},{5,4},{6,5},{7,6},{9,8},{10,9},{11,10},{12... | collective-permute-start | bytes 12680 | tf_op jit(solution)/shard_map/ppermute | solution.py:19
  226.1 3.8 copy-start.3
  229.8 1.9 copy-start.6
  249.6 4.5 copy-start.15
  249.6 4.5 copy-start.16
  251.5 2.6 copy-start.7
  251.5 2.6 copy-start.14
  251.6 2.6 copy-start.26
  251.6 2.6 copy-start.29
  263.6 7.5 %copy-start.18 = (bf16[32,65,256]{2,0,1:T(8,128)(2,1)S(1)}, bf16[32,65,256]{2,0,1:T(8,128)(2,1)}, u32[]{:S(2)}) copy-start(bf16[32,65,256]{2,0,1:T(8,128)(2,1)} %copy-done.17) | copy-start | bytes 3194884
  264.2 334.4 %collective-permute-start.5 = (bf16[32,1,256]{2,0,1:T(8,128)(2,1)}, bf16[32,1,256]{2,0,1:T(8,128)(2,1)S(1)}, u32[]{:S(2)}, u32[]{:S(2)}) collective-permute-start(bf16[32,1,256]{2,0,1:T(8,128)(2,1)} %get-tuple-element.57), channel_id=1, source_target_pairs={{8,0},{16,8},{24,16},{32,24},{40,32},{48,40},{56,48},{64,56},{72,6... | collective-permute-start | bytes 49160 | tf_op jit(solution)/shard_map/ppermute | solution.py:19
  266.1 6.0 copy-start.8
  266.1 332.5 %collective-permute-start.4 = (bf16[32,1,256]{2,0,1:T(8,128)(2,1)}, bf16[32,1,256]{2,0,1:T(8,128)(2,1)}, u32[]{:S(2)}, u32[]{:S(2)}) collective-permute-start(bf16[32,1,256]{2,0,1:T(8,128)(2,1)} %get-tuple-element.58), channel_id=1, source_target_pairs={{0,8},{8,16},{16,24},{24,32},{32,40},{40,48},{48,56},{56,64},{64,7... | collective-permute-start | bytes 49160 | tf_op jit(solution)/shard_map/ppermute | solution.py:18
  272.1 1.3 copy-start.4
  323.3 20.5 %all-to-all-start.2 = ((f32[32,1,2048]{2,1,0:T(1,128)}), f32[32,1,2048]{2,1,0:T(1,128)}, u32[]{:S(2)}, u32[]{:S(2)}) async-start(f32[32,1,2048]{2,1,0:T(1,128)} %reshape.253), calls=%async_computation.4 | async-start | bytes 524288 | tf_op jit(solution)/shard_map/all_to_all | solution.py:175
  332.6 199.5 %reduce-scatter.15.cloned.1.call-start = ((), (), s32[]{:S(2)}) async-start(), calls=%async_computation.13 | async-start | bytes 294912
  332.6 1.4 copy-start.9
  334.1 1.3 copy-start.5
  351.7 6.1 copy-start.2
  357.8 1.1 copy-start.10
  357.8 2.4 copy-start.27
  357.8 2.3 copy-start.28
  570.0 13.1 %copy-start.24 = (f32[3,3,32,32]{3,2,1,0:T(8,128)S(1)}, f32[3,3,32,32]{3,2,1,0:T(8,128)}, u32[]{:S(2)}) copy-start(f32[3,3,32,32]{3,2,1,0:T(8,128)} %get-tuple-element.44) | copy-start | bytes 110596
  572.6 21.3 %all-to-all-start.3 = ((f32[32,1,2048]{2,1,0:T(1,128)}), f32[32,1,2048]{2,1,0:T(1,128)S(1)}, u32[]{:S(2)}, u32[]{:S(2)}) async-start(f32[32,1,2048]{2,1,0:T(1,128)} %reshape.255), calls=%async_computation.5 | async-start | bytes 524288 | tf_op jit(solution)/shard_map/all_to_all | solution.py:187
  583.0 64.6 %all-gather.5.cloned.1.call-start = ((), (), s32[]{:S(2)}) async-start(), calls=%async_computation.11 | async-start | bytes 2359296 | tf_op jit(solution)/shard_map/all_gather | solution.py:189
  598.6 11.1 %copy-start.23 = (bf16[32,1,256]{2,0,1:T(8,128)(2,1)}, bf16[32,1,256]{2,0,1:T(8,128)(2,1)S(1)}, u32[]{:S(2)}) copy-start(bf16[32,1,256]{2,0,1:T(8,128)(2,1)S(1)} %collective-permute-done.5) | copy-start | bytes 49156
  601.1 11.3 %collective-permute-start.6 = (bf16[32,66,1]{1,0,2:T(8,128)(2,1)S(1)}, bf16[32,66,1]{1,0,2:T(8,128)(2,1)S(1)}, u32[]{:S(2)}, u32[]{:S(2)}) collective-permute-start(bf16[32,66,1]{1,0,2:T(8,128)(2,1)S(1)} %copy.238), channel_id=1, source_target_pairs={{1,0},{2,1},{3,2},{4,3},{5,4},{6,5},{7,6},{9,8},{10,9},{11,10},{12... | collective-permute-start | bytes 12680 | tf_op jit(solution)/shard_map/ppermute | solution.py:19
  602.4 9.0 %collective-permute-start.7 = (bf16[32,66,1]{1,0,2:T(8,128)(2,1)S(1)}, bf16[32,66,1]{1,0,2:T(8,128)(2,1)S(1)}, u32[]{:S(2)}, u32[]{:S(2)}) collective-permute-start(bf16[32,66,1]{1,0,2:T(8,128)(2,1)S(1)} %copy.242), channel_id=1, source_target_pairs={{0,1},{1,2},{2,3},{3,4},{4,5},{5,6},{6,7},{8,9},{9,10},{10,11},{11... | collective-permute-start | bytes 12680 | tf_op jit(solution)/shard_map/ppermute | solution.py:18
  623.6 1.8 copy-start.20
  623.6 1.8 copy-start.21
  623.6 1.8 copy-start.22
  647.6 4.2 copy-start.11
  647.6 4.2 copy-start.12
Sparse Core Ops, SparseCore 0:
  11.4 58.0 reduce-scatter.8
  102.9 35.4 reduce-scatter.12
  200.0 49.5 all-gather.2
  263.7 54.8 reduce-scatter.10
  357.9 35.6 reduce-scatter.14
  597.7 49.8 all-gather.4
